TPU v7x, 32 devices: a whole 2x2x4 slice. The times are simulated.
32 devices in a mesh: region: 4 (over y, x), tile: 8 (over z, core).
Axes of the slice: x: 2, y: 2, z: 4, core: 2. Of those that a mesh axis runs over, the one named last changes fastest.
Arguments:
- right_side: float32 [16, 32, 32, 256], P('region', 'tile'), may hold values from -20 to 20
- coords: float32 [16, 32, 2, 256], P('region', 'tile'), may hold values from 0 to 1
- pair_list: int32 [8, 16, 32], P(None, 'region', 'tile'), may hold values from 0 to 1, as said below
Outputs:
- solution: float32 [16, 32, 32, 256], P('region', 'tile')
- residual: float32 [16, 32, 32, 256], P('region', 'tile')
Inputs may be any that keep to these rules, and one draw needn't show every extreme that they name: pair_list[k + 4] at a block equals pair_list[k] at its neighbour in direction k + 4, for k < 4; a direction that leaves the grid of 16 x 32 blocks is 0.
All inputs are finite; a program needn't handle non-finite values.
Results may differ from a plain program's by a relative error of at most 0.0003.
Values sent between devices are 32-bit elements; how exact they have to be, the bound alone decides.
No kernel may reach another device: no remote copies, remote signals or barrier semaphores. Data moves between devices by JAX's collectives and lax.ppermute only.
A program may use at most 64 MiB of HBM per device.

v0:
```python
import functools

import jax
import jax.numpy as jnp
from jax import lax
from jax.experimental import pallas as pl
from jax.experimental.pallas import tpu as pltpu
from jax.sharding import PartitionSpec as P

LENGTH_SCALE = 0.2
TAPER_RANGE = 0.5
NUGGET = 3.0
OFFSETS = ((0, 1), (1, 0), (1, 1), (1, -1), (0, -1), (-1, 0), (-1, -1), (-1, 1))
UNIT = 1.4426950408889634 / LENGTH_SCALE
EDGE = UNIT * TAPER_RANGE
WEIGHT = 4.0 * 2.0**-EDGE / EDGE**5
STRIP = 64
LONG_TURN_LOG2 = 3
VMEM_LIMIT = 10 * 1024 * 1024


def dot_nn(a, b):
    return lax.dot_general(a, b, (((1,), (0,)), ((), ())), preferred_element_type=jnp.float32)


def dot_nt(a, b):
    return lax.dot_general(a, b, (((1,), (1,)), ((), ())), preferred_element_type=jnp.float32)


def split_hi_lo(values):
    hi = values.astype(jnp.bfloat16)
    lo = (values - hi.astype(jnp.float32)).astype(jnp.bfloat16)
    return hi, lo


def across_lanes(row, lanes):
    return jnp.transpose(jnp.broadcast_to(row, (lanes, row.shape[1])))


def make_tile(keep_ref, slot, spread_ref, down, points_ref, along, shift_a, shift_b):
    points = keep_ref.shape[2]
    lanes = spread_ref.shape[3]
    row_x = points_ref[along, 0:1] - shift_a
    row_y = points_ref[along, 1:2] - shift_b
    for start in range(0, points, STRIP):
        rows = slice(start, start + STRIP)
        for left in range(0, points, lanes):
            cols = slice(left, left + lanes)
            gap_x = spread_ref[down, 0, rows] - row_x[:, cols]
            gap_y = spread_ref[down, 1, rows] - row_y[:, cols]
            square = jnp.maximum(gap_x * gap_x + gap_y * gap_y, 1e-30)
            rest = jnp.maximum(EDGE - square * lax.rsqrt(square), 0.0)
            rest2 = rest * rest
            cov = (jnp.exp2(rest) * (rest2 * rest2)) * (1.25 * EDGE - rest)
            for part, values in enumerate(split_hi_lo(cov)):
                keep_ref[slot, part, rows, cols] = values


def product(dot, parts_ref, at, high, low):
    rhs = parts_ref.shape[1] // 2
    both = dot(parts_ref[at], high)
    cross = dot(parts_ref[at, 0:rhs], low)
    return both[:rhs] + both[rhs:] + cross


def store_parts(parts_ref, at, values):
    rhs = values.shape[0]
    hi, lo = split_hi_lo(values * WEIGHT)
    parts_ref[at, 0:rhs] = hi
    parts_ref[at, rhs : 2 * rhs] = lo


def in_turns(count, step):
    turns = lax.shift_right_logical(count + 1, 1)

    def one_turn(turn, carry):
        step(2 * turn)
        step(2 * turn + 1)
        return carry

    lax.fori_loop(0, turns, one_turn, 0)


def only_use(count, kept_ref, base, use):
    def one_turn(start, length):
        for n in range(length):
            use(kept_ref[base + start + n, 0], kept_ref[base + start + n, 1], start + n)

    whole = lax.shift_right_logical(count, LONG_TURN_LOG2)
    lax.fori_loop(0, whole, lambda turn, c: (one_turn(turn << LONG_TURN_LOG2, 1 << LONG_TURN_LOG2), c)[1], 0)
    lax.fori_loop(whole << LONG_TURN_LOG2, count, lambda n, c: (one_turn(n, 1), c)[1], 0)


def item_code(own, other, shift_a, shift_b):
    return own + 64 * other + 4096 * (shift_a + 1) + 16384 * (shift_b + 1)


NO_ITEM = item_code(0, 0, 2, 2)


def item_blocks(code):
    return lax.bitwise_and(code, 63), lax.bitwise_and(lax.shift_right_logical(code, 6), 63)


def item_shifts(code):
    shift_a = lax.bitwise_and(lax.shift_right_logical(code, 12), 3) - 1
    shift_b = lax.shift_right_logical(code, 14) - 1
    return shift_a.astype(jnp.float32) * UNIT, shift_b.astype(jnp.float32) * UNIT


def list_items(items_ref, candidates, pair_ref):
    cols = pair_ref.shape[2]
    count = jnp.int32(0)
    for k, own, code in candidates:
        items_ref[count + 1] = code
        count = count + jnp.where(pair_ref[k, own // cols, own % cols] > 0, 1, 0)
    items_ref[0] = count
    items_ref[count + 1] = NO_ITEM


def inner_candidates(rows, cols):
    found = []
    for k in range(4):
        shift_a, shift_b = OFFSETS[k]
        for a in range(rows):
            for b in range(cols):
                if 0 <= a + shift_a < rows and 0 <= b + shift_b < cols:
                    own = a * cols + b
                    other = own + shift_a * cols + shift_b
                    found.append((k, own, item_code(own, other, shift_a, shift_b)))
    return found


def cross_candidates(rows, cols):
    places = [(a, -1) for a in range(rows)] + [(a, cols) for a in range(rows)]
    places += [(-1, b) for b in range(-1, cols + 1)] + [(rows, b) for b in range(-1, cols + 1)]
    found = []
    for k in range(8):
        shift_a, shift_b = OFFSETS[k]
        for a in range(rows):
            for b in range(cols):
                place = (a + shift_a, b + shift_b)
                if place in places:
                    own = a * cols + b
                    found.append((k, own, item_code(own, places.index(place), -shift_a, -shift_b)))
    return found


def pack_kernel(v_ref, c_ref, first_ref, last_ref, edge_ref, v_out_ref, c_out_ref):
    rows, cols, rhs = v_ref.shape[:3]
    both = slice(rhs, rhs + 2)
    for column_ref, at in ((first_ref, 0), (last_ref, cols - 1)):
        column_ref[:, 0:rhs] = v_ref[:, at]
        column_ref[:, both] = c_ref[:, at]
    for n, at in enumerate((0, rows - 1)):
        edge_ref[n, :, 0:rhs] = v_ref[at]
        edge_ref[n, :, both] = c_ref[at]
    for row in range(rows):
        v_out_ref[row * cols : (row + 1) * cols] = v_ref[row]
        c_out_ref[row * cols : (row + 1) * cols] = c_ref[row]


def prepare_kernel(pair_ref, v_ref, c_ref, near_ref, cross_ref, parts_ref, points_ref, spread_ref):
    rows, cols = pair_ref.shape[1:]
    lanes = spread_ref.shape[3]

    def one(at, carry):
        store_parts(parts_ref, at, v_ref[at])
        scaled = c_ref[at] * UNIT
        points_ref[at] = scaled
        for axis in range(2):
            spread_ref[at, axis] = across_lanes(scaled[axis : axis + 1], lanes)
        return carry

    lax.fori_loop(0, rows * cols, one, 0, unroll=2)
    list_items(near_ref, inner_candidates(rows, cols), pair_ref)
    list_items(cross_ref, cross_candidates(rows, cols), pair_ref)


def use_own(out_ref, parts_ref, high, low, at):
    out_ref[at] += product(dot_nn, parts_ref, at, high, low)


def use_pair(out_ref, parts_ref, items_ref, high, low, n):
    own, other = item_blocks(items_ref[n + 1])
    out_ref[own] += product(dot_nn, parts_ref, other, high, low)
    out_ref[other] += product(dot_nt, parts_ref, own, high, low)


def use_cross(out_ref, parts_ref, items_ref, high, low, n):
    own, other = item_blocks(items_ref[n + 1])
    out_ref[own] += product(dot_nt, parts_ref, other, high, low)


def near_first_kernel(items_ref, v_ref, parts_ref, points_ref, spread_ref, out_ref, kept_ref):
    blocks = parts_ref.shape[0]
    out_ref[...] = NUGGET * v_ref[...]

    def make_own(at):
        make_tile(kept_ref, at, spread_ref, at, points_ref, at, 0.0, 0.0)

    def make_pair(n):
        code = items_ref[n + 1]
        own, other = item_blocks(code)
        make_tile(kept_ref, blocks + n, spread_ref, other, points_ref, own, *item_shifts(code))

    in_turns(jnp.int32(blocks), make_own)
    in_turns(items_ref[0], make_pair)
    only_use(jnp.int32(blocks), kept_ref, 0, functools.partial(use_own, out_ref, parts_ref))
    only_use(items_ref[0], kept_ref, blocks, functools.partial(use_pair, out_ref, parts_ref, items_ref))


def take_round(round_refs, rhs, parts_ref, points_ref=None):
    start = 0
    for side in round_refs:

        def take(at, carry, side=side, start=start):
            store_parts(parts_ref, start + at, side[at, 0:rhs])
            if points_ref is not None:
                points_ref[start + at] = side[at, rhs : rhs + 2] * UNIT
            return carry

        lax.fori_loop(0, side.shape[0], take, 0)
        start += side.shape[0]


def cross_first_kernel(
    items_ref, sum_ref, west_ref, east_ref, north_ref, south_ref, spread_ref,
    out_ref, kept_ref, parts_ref, points_ref
):
    out_ref[...] = sum_ref[...]
    take_round((west_ref, east_ref, north_ref, south_ref), sum_ref.shape[1], parts_ref, points_ref)

    def make(n):
        code = items_ref[n + 1]
        own, other = item_blocks(code)
        make_tile(kept_ref, n, spread_ref, own, points_ref, other, *item_shifts(code))

    in_turns(items_ref[0], make)
    only_use(items_ref[0], kept_ref, 0, functools.partial(use_cross, out_ref, parts_ref, items_ref))


def own_again_kernel(v_ref, kept_ref, out_ref, parts_ref):
    def one(at, carry):
        store_parts(parts_ref, at, v_ref[at])
        out_ref[at] = NUGGET * v_ref[at]
        return carry

    lax.fori_loop(0, parts_ref.shape[0], one, 0, unroll=2)
    only_use(jnp.int32(parts_ref.shape[0]), kept_ref, 0, functools.partial(use_own, out_ref, parts_ref))


def inner_again_kernel(items_ref, sum_ref, parts_ref, kept_ref, out_ref):
    out_ref[...] = sum_ref[...]
    use = functools.partial(use_pair, out_ref, parts_ref, items_ref)
    only_use(items_ref[0], kept_ref, parts_ref.shape[0], use)


def cross_again_kernel(
    items_ref, sum_ref, west_ref, east_ref, north_ref, south_ref, kept_ref, v0_ref, v1_ref,
    out_ref, moments_ref, parts_ref
):
    out_ref[...] = sum_ref[...]
    take_round((west_ref, east_ref, north_ref, south_ref), sum_ref.shape[1], parts_ref)
    only_use(items_ref[0], kept_ref, 0, functools.partial(use_cross, out_ref, parts_ref, items_ref))
    zero = jnp.zeros(out_ref.shape[1:], jnp.float32)

    def gather(at, sums):
        w0, w1, w2 = v0_ref[at], v1_ref[at], out_ref[at]
        terms = (w0 * w0, w0 * w1, w1 * w1, w1 * w2)
        return tuple(s + t for s, t in zip(sums, terms))

    sums = lax.fori_loop(0, out_ref.shape[0], gather, (zero,) * 4)
    lanes = moments_ref.shape[2]
    folded = [sum(s[:, left : left + lanes] for left in range(0, s.shape[1], lanes)) for s in sums]
    stacked = jnp.concatenate(folded, axis=0)
    line = jnp.sum(jnp.transpose(stacked), axis=0, keepdims=True)
    moments_ref[...] = jnp.broadcast_to(line[None], moments_ref.shape)


def final_kernel(moments_ref, v0_ref, v1_ref, v2_ref, solution_ref, residual_ref):
    rhs, points = v0_ref.shape[1:]
    line = moments_ref[0]
    for at in range(1, moments_ref.shape[0]):
        line = line + moments_ref[at]
    table = across_lanes(line, line.shape[1])
    m00, m01, m11, m12 = (table[k * rhs : (k + 1) * rhs] for k in range(4))
    a = m00 / m01
    norm = m00 - 2.0 * a * m01 + a * a * m11
    grow = 1.0 + norm / m00
    step = norm / (grow * (grow * m01 - 2.0 * a * m11) + a * a * m12)
    first = jnp.concatenate([a + step * grow] * (points // line.shape[1]), axis=1)
    second = jnp.concatenate([step * a] * (points // line.shape[1]), axis=1)

    def one(at, carry):
        w0, w1, w2 = v0_ref[at], v1_ref[at], v2_ref[at]
        solution_ref[at] = first * w0 - second * w1
        residual_ref[at] = w0 - first * w1 + second * w2
        return carry

    lax.fori_loop(0, v0_ref.shape[0], one, 0)


def swapped(first, last, axis):
    count = lax.axis_size(axis)
    even = lax.rem(lax.axis_index(axis), 2) == 0
    swap_up = [(i, i ^ 1) for i in range(count) if i ^ 1 < count]
    swap_down = [(i, ((i + 1) ^ 1) - 1) for i in range(count) if 0 <= ((i + 1) ^ 1) - 1 < count]
    got_up = lax.ppermute(jnp.where(even, last, first), axis, swap_up)
    got_down = lax.ppermute(jnp.where(even, first, last), axis, swap_down)
    return jnp.where(even, got_down, got_up), jnp.where(even, got_up, got_down)


def on_device(kernel, outputs, inputs, scratch=(), listed=False, products=0, made=0):
    vmem = pl.BlockSpec(memory_space=pltpu.VMEM)
    smem = pl.BlockSpec(memory_space=pltpu.SMEM)
    return pl.pallas_call(
        kernel,
        out_shape=tuple(outputs),
        in_specs=[smem if listed and n == 0 else vmem for n in range(len(inputs))],
        out_specs=tuple(smem if out.dtype == jnp.int32 else vmem for out in outputs),
        scratch_shapes=list(scratch),
        compiler_params=pltpu.CompilerParams(vmem_limit_bytes=VMEM_LIMIT),
        cost_estimate=pl.CostEstimate(
            flops=products, transcendentals=made, bytes_accessed=sum(4 * x.size for x in inputs)
        ),
        name=kernel.__name__,
    )(*inputs)


def tiles(count, points):
    return jax.ShapeDtypeStruct((count, 2, points, points), jnp.bfloat16)


def per_device(right_side, coords, pair_list):
    rows, cols, rhs, points = right_side.shape
    blocks = rows * cols
    devices = lax.axis_size("region") * lax.axis_size("tile")
    lanes = 128
    f32, bf16, i32 = jnp.float32, jnp.bfloat16, jnp.int32
    array = jax.ShapeDtypeStruct
    halo = 2 * rows + 2 * (cols + 2)
    near_count = len(inner_candidates(rows, cols))
    cross_count = len(cross_candidates(rows, cols))
    field = array((blocks, rhs, points), f32)
    column = array((rows, rhs + 2, points), f32)
    parts_round = pltpu.VMEM((halo, 2 * rhs, points), bf16)
    each = 6 * rhs * points * points

    def rows_round(first, last, west, east):
        top = jnp.concatenate([west[:1], first, east[:1]], axis=0)
        bottom = jnp.concatenate([west[rows - 1 :], last, east[rows - 1 :]], axis=0)
        return swapped(top, bottom, "region")

    first, last, edges, w0, stations = on_device(
        pack_kernel, (column, column, array((2, cols, rhs + 2, points), f32), field, array((blocks, 2, points), f32)),
        (right_side, coords),
    )
    west, east = swapped(first, last, "tile")
    near_items, cross_items, parts, own_points, spread = on_device(
        prepare_kernel,
        (array((near_count + 3,), i32), array((cross_count + 3,), i32), array((blocks, 2 * rhs, points), bf16),
         array((blocks, 2, points), f32), array((blocks, 2, points, lanes), f32)),
        (pair_list, w0, stations), listed=True, products=blocks * each,
    )
    west, east, parts = lax.optimization_barrier((west, east, parts))
    north, south = rows_round(edges[0], edges[1], west, east)
    part, near_tiles = on_device(
        near_first_kernel, (field, tiles(blocks + near_count + 2, points)),
        (near_items, w0, parts, own_points, spread), (), True,
        (blocks + near_count) * each, (blocks + near_count) * 2 * points * points,
    )
    w1, cross_tiles = on_device(
        cross_first_kernel, (field, tiles(cross_count + 2, points)),
        (cross_items, part, west, east, north, south, spread),
        (parts_round, pltpu.VMEM((halo, 2, points), f32)), True,
        cross_count * each, cross_count * 2 * points * points,
    )
    w1_grid = w1.reshape(right_side.shape)
    west, east = swapped(w1_grid[:, 0], w1_grid[:, cols - 1], "tile")
    part, parts = on_device(
        own_again_kernel, (field, array((blocks, 2 * rhs, points), bf16)), (w1, near_tiles), products=blocks * each
    )
    west, east, part = lax.optimization_barrier((west, east, part))
    north, south = rows_round(w1_grid[0], w1_grid[rows - 1], west, east)
    (part,) = on_device(
        inner_again_kernel, (field,), (near_items, part, parts, near_tiles), (), True, near_count * each
    )
    w2, moments = on_device(
        cross_again_kernel, (field, array((devices, 1, 4 * rhs), f32)),
        (cross_items, part, west, east, north, south, cross_tiles, w0, w1), (parts_round,), True, cross_count * each,
    )
    moments = lax.all_to_all(moments, ("region", "tile"), 0, 0)
    solution, residual = on_device(final_kernel, (field, field), (moments, w0, w1, w2))
    return solution.reshape(right_side.shape), residual.reshape(right_side.shape)


def solution(mesh):
    placed = (
        P("region", "tile", None, None),
        P("region", "tile", None, None),
        P(None, "region", "tile"),
    )
    return jax.shard_map(
        per_device,
        mesh=mesh,
        in_specs=placed,
        out_specs=(P("region", "tile", None, None), P("region", "tile", None, None)),
        check_vma=False,
    )
```

profile of v0, /device:TPU:0, one launch (start us, length us, event | category | flops | bytes accessed | tf_op | source)
XLA Modules:
  0.0 74.0 jit_solution(5284223002073359122)
XLA Ops:
  0.6 0.0 copy-start
  0.6 1.0 %copy-done = f32[4,4,32,256]{3,2,1,0:T(8,128)S(1)} copy-done((f32[4,4,32,256]{3,2,1,0:T(8,128)S(1)}, f32[4,4,32,256]{3,2,1,0:T(8,128)}, u32[]{:S(2)}) %copy-start) | copy-done | bytes 524312
  1.7 0.0 copy-start.1
  1.7 0.8 %copy-done.1 = f32[4,4,2,256]{3,2,1,0:T(2,128)S(1)} copy-done((f32[4,4,2,256]{3,2,1,0:T(2,128)S(1)}, f32[4,4,2,256]{3,2,1,0:T(2,128)}, u32[]{:S(2)}) %copy-start.1) | copy-done | bytes 32792
  2.4 0.1 pack_kernel.1
  2.6 0.6 collective-permute-start.1
  3.1 0.7 collective-permute-start
  3.8 0.8 %copy.6.pair_ref = s32[8,4,4]{2,1,0:T(4,128)S(1)} copy(s32[8,4,4]{0,2,1:T(4,128)} %param.5) | data formatting | bytes 1024 | tf_op args[2]
  4.6 3.3 %prepare_kernel.1 = (s32[45]{0:T(128)S(1)}, s32[47]{0:T(128)S(1)}, bf16[16,64,256]{2,1,0:T(8,128)(2,1)S(1)}, f32[16,2,256]{2,1,0:T(2,128)S(1)}, f32[16,2,256,128]{3,2,1,0:T(8,128)S(1)}) custom-call(s32[8,4,4]{2,1,0:T(4,128)S(1)} %copy.6.pair_ref, f32[16,32,256]{2,1,0:T(8,128)S(1)} %get-tuple-element.28.v_ref.v0_ref, f32[16,2,256]{2,1,0:T(2,128)S(1)} %get-tuple-element.29.c_ref), custom_call_target="tpu_custom_call" | custom-call | flops 201326592 | bytes 557568 | tf_op jit(solution)/shard_map/prepare_kernel/pallas_call | solution.py:317
  7.9 0.0 collective-permute-done.1
  7.9 0.0 collective-permute-done
  8.0 2.6 %collective-permute-start.3 = (f32[6,34,256]{2,1,0:T(8,128)S(1)}, f32[6,34,256]{2,1,0:T(8,128)S(1)}, u32[]{:S(2)}, u32[]{:S(2)}) collective-permute-start(f32[6,34,256]{2,1,0:T(8,128)S(1)} %get-tuple-element.60), channel_id=1, source_target_pairs={{0,8},{8,0},{16,24},{24,16},{1,9},{9,1},{17,25},{25,17},{2,10},{10... | collective-permute-start | bytes 626696 | tf_op jit(solution)/shard_map/ppermute | solution.py:309
  10.6 0.7 collective-permute-start.2
  11.3 7.7 %near_first_kernel.1 = (f32[16,32,256]{2,1,0:T(8,128)S(1)}, bf16[60,2,256,256]{3,2,1,0:T(8,128)(2,1)S(1)}) custom-call(s32[45]{0:T(128)S(1)} %get-tuple-element.31.items_ref, f32[16,32,256]{2,1,0:T(8,128)S(1)} %get-tuple-element.28.v_ref.v0_ref, bf16[16,64,256]{2,1,0:T(8,128)(2,1)S(1)} %get-tuple-element.35.parts_ref, ...), custom_call_target="tpu_custom_call" | custom-call | flops 729808896 | bytes 5800116 | tf_op jit(solution)/shard_map/near_first_kernel/pallas_call | solution.py:317
  19.0 0.0 collective-permute-done.3
  19.0 0.0 collective-permute-done.2
  19.1 2.1 %cross_first_kernel.1 = (f32[16,32,256]{2,1,0:T(8,128)S(1)}, bf16[46,2,256,256]{3,2,1,0:T(8,128)(2,1)S(1)}) custom-call(s32[47]{0:T(128)S(1)} %get-tuple-element.30.items_ref, f32[16,32,256]{2,1,0:T(8,128)S(1)} %get-tuple-element.38.sum_ref, f32[4,34,256]{2,1,0:T(8,128)S(1)} %get-tuple-element.39.west_ref, f32[4,34,256]{2,1,0:T(8,128)S(1)} %get-tuple-element.40.east_ref, ...), custom_call_target="tpu_custom_call" | custom-call | flops 553648128 | bytes 5415100 | tf_op jit(solution)/shard_map/cross_first_kernel/pallas_call | solution.py:317
  21.2 2.1 %collective-permute-start.5 = (f32[4,32,256]{2,1,0:T(8,128)S(1)}, f32[4,32,256]{2,1,0:T(8,128)S(1)}, u32[]{:S(2)}, u32[]{:S(2)}) collective-permute-start(f32[4,32,256]{2,1,0:T(8,128)S(1)} %get-tuple-element.56), channel_id=1, source_target_pairs={{0,1},{1,0},{2,3},{3,2},{4,5},{5,4},{6,7},{7,6},{8,9},{9,8},{10,11... | collective-permute-start | bytes 393224 | tf_op jit(solution)/shard_map/ppermute | solution.py:309
  23.3 0.7 collective-permute-start.4
  24.0 1.0 %own_again_kernel.1 = (f32[16,32,256]{2,1,0:T(8,128)S(1)}, bf16[16,64,256]{2,1,0:T(8,128)(2,1)S(1)}) custom-call(f32[16,32,256]{2,1,0:T(8,128)S(1)} %get-tuple-element.42.v_ref.v1_ref, bf16[60,2,256,256]{3,2,1,0:T(8,128)(2,1)S(1)} %get-tuple-element.43.kept_ref), custom_call_target="tpu_custom_call" | custom-call | flops 201326592 | bytes 31981568 | tf_op jit(solution)/shard_map/own_again_kernel/pallas_call | solution.py:317
  25.0 0.0 collective-permute-done.5
  25.0 0.0 collective-permute-done.4
  25.1 7.0 %collective-permute-start.7 = (f32[6,32,256]{2,1,0:T(8,128)S(1)}, f32[6,32,256]{2,1,0:T(8,128)S(1)}, u32[]{:S(2)}, u32[]{:S(2)}) collective-permute-start(f32[6,32,256]{2,1,0:T(8,128)S(1)} %get-tuple-element.64), channel_id=1, source_target_pairs={{0,8},{8,0},{16,24},{24,16},{1,9},{9,1},{17,25},{25,17},{2,10},{10... | collective-permute-start | bytes 589832 | tf_op jit(solution)/shard_map/ppermute | solution.py:309
  32.1 0.7 collective-permute-start.6
  32.8 2.4 %inner_again_kernel.1.sum_ref = f32[16,32,256]{2,1,0:T(8,128)S(1)} custom-call(s32[45]{0:T(128)S(1)} %get-tuple-element.31.items_ref, f32[16,32,256]{2,1,0:T(8,128)S(1)} %get-tuple-element.45.sum_ref, bf16[16,64,256]{2,1,0:T(8,128)(2,1)S(1)} %get-tuple-element.46.parts_ref, bf16[60,2,256,256]{3,2,1,0:T(8,128)(2,1)S(1)} %get-tuple-element.43.kept_ref), custom_call_target="tpu_custom_call" | custom-call | flops 528482304 | bytes 33030324 | tf_op jit(solution)/shard_map/inner_again_kernel/pallas_call | solution.py:317
  35.2 0.5 collective-permute-done.7
  35.7 0.0 collective-permute-done.6
  35.8 1.8 %cross_again_kernel.1 = (f32[16,32,256]{2,1,0:T(8,128)S(1)}, f32[32,1,128]{2,1,0:T(1,128)S(1)}) custom-call(s32[47]{0:T(128)S(1)} %get-tuple-element.30.items_ref, f32[16,32,256]{2,1,0:T(8,128)S(1)} %inner_again_kernel.1.sum_ref, f32[4,32,256]{2,1,0:T(8,128)S(1)} %get-tuple-element.47.west_ref, f32[4,32,256]{2,1,0:T(8,128)S(1)} %get-tuple-element.48.east_ref, ...), custom_call_target="tpu_custom_call" | custom-call | flops 553648128 | bytes 26345660 | tf_op jit(solution)/shard_map/cross_again_kernel/pallas_call | solution.py:317
  37.6 35.0 %all_to_all.5.moments_ref = f32[32,1,128]{2,1,0:T(1,128)S(1)} all-to-all(f32[32,1,128]{2,1,0:T(1,128)S(1)} %get-tuple-element.50), channel_id=1, replica_groups=mesh['region'=4,'tile'=8] {'region','tile'}, dimensions={0} | all-to-all | bytes 32768 | tf_op jit(solution)/shard_map/all_to_all | solution.py:393
  72.7 1.3 %final_kernel.1 = (f32[16,32,256]{2,1,0:T(8,128)}, f32[16,32,256]{2,1,0:T(8,128)}) custom-call(f32[32,1,128]{2,1,0:T(1,128)S(1)} %all_to_all.5.moments_ref, f32[16,32,256]{2,1,0:T(8,128)S(1)} %get-tuple-element.28.v_ref.v0_ref, f32[16,32,256]{2,1,0:T(8,128)S(1)} %get-tuple-element.42.v_ref.v1_ref, f32[16,32,256]{2,1,0:T(8,128)S(1)} %get-tuple-element.51.v2_ref), custom_call_target="tpu_custom_call" | custom-call | bytes 1589248 | tf_op jit(solution)/shard_map/final_kernel/pallas_call | solution.py:317
  (13 shorter events, 0.3 us)
Async XLA Ops:
  0.6 1.0 %copy-start = (f32[4,4,32,256]{3,2,1,0:T(8,128)S(1)}, f32[4,4,32,256]{3,2,1,0:T(8,128)}, u32[]{:S(2)}) copy-start(f32[4,4,32,256]{3,2,1,0:T(8,128)} %v_ref.1) | copy-start | bytes 1572868
  1.7 0.8 %copy-start.1 = (f32[4,4,2,256]{3,2,1,0:T(2,128)S(1)}, f32[4,4,2,256]{3,2,1,0:T(2,128)}, u32[]{:S(2)}) copy-start(f32[4,4,2,256]{3,2,1,0:T(2,128)} %c_ref.1) | copy-start | bytes 98308
  2.6 5.4 %collective-permute-start.1 = (f32[4,34,256]{2,1,0:T(8,128)S(1)}, f32[4,34,256]{2,1,0:T(8,128)S(1)}, u32[]{:S(2)}, u32[]{:S(2)}) collective-permute-start(f32[4,34,256]{2,1,0:T(8,128)S(1)} %get-tuple-element.70), channel_id=1, source_target_pairs={{0,1},{1,0},{2,3},{3,2},{4,5},{5,4},{6,7},{7,6},{8,9},{9,8},{10,11... | collective-permute-start | bytes 417800 | tf_op jit(solution)/shard_map/ppermute | solution.py:309
  3.1 4.8 %collective-permute-start = (f32[4,34,256]{2,1,0:T(8,128)S(1)}, f32[4,34,256]{2,1,0:T(8,128)S(1)}, u32[]{:S(2)}, u32[]{:S(2)}) collective-permute-start(f32[4,34,256]{2,1,0:T(8,128)S(1)} %get-tuple-element.71), channel_id=1, source_target_pairs={{1,2},{2,1},{3,4},{4,3},{5,6},{6,5},{9,10},{10,9},{11,12},{12,11},... | collective-permute-start | bytes 417800 | tf_op jit(solution)/shard_map/ppermute | solution.py:310
  8.0 10.9 %collective-permute-start.3 = (f32[6,34,256]{2,1,0:T(8,128)S(1)}, f32[6,34,256]{2,1,0:T(8,128)S(1)}, u32[]{:S(2)}, u32[]{:S(2)}) collective-permute-start(f32[6,34,256]{2,1,0:T(8,128)S(1)} %get-tuple-element.60), channel_id=1, source_target_pairs={{0,8},{8,0},{16,24},{24,16},{1,9},{9,1},{17,25},{25,17},{2,10},{10... | collective-permute-start | bytes 626696 | tf_op jit(solution)/shard_map/ppermute | solution.py:309
  10.6 8.4 %collective-permute-start.2 = (f32[6,34,256]{2,1,0:T(8,128)S(1)}, f32[6,34,256]{2,1,0:T(8,128)S(1)}, u32[]{:S(2)}, u32[]{:S(2)}) collective-permute-start(f32[6,34,256]{2,1,0:T(8,128)S(1)} %get-tuple-element.61), channel_id=1, source_target_pairs={{8,16},{16,8},{9,17},{17,9},{10,18},{18,10},{11,19},{19,11},{12,20... | collective-permute-start | bytes 626696 | tf_op jit(solution)/shard_map/ppermute | solution.py:310
  21.2 3.8 %collective-permute-start.5 = (f32[4,32,256]{2,1,0:T(8,128)S(1)}, f32[4,32,256]{2,1,0:T(8,128)S(1)}, u32[]{:S(2)}, u32[]{:S(2)}) collective-permute-start(f32[4,32,256]{2,1,0:T(8,128)S(1)} %get-tuple-element.56), channel_id=1, source_target_pairs={{0,1},{1,0},{2,3},{3,2},{4,5},{5,4},{6,7},{7,6},{8,9},{9,8},{10,11... | collective-permute-start | bytes 393224 | tf_op jit(solution)/shard_map/ppermute | solution.py:309
  23.3 1.7 %collective-permute-start.4 = (f32[4,32,256]{2,1,0:T(8,128)S(1)}, f32[4,32,256]{2,1,0:T(8,128)S(1)}, u32[]{:S(2)}, u32[]{:S(2)}) collective-permute-start(f32[4,32,256]{2,1,0:T(8,128)S(1)} %get-tuple-element.57), channel_id=1, source_target_pairs={{1,2},{2,1},{3,4},{4,3},{5,6},{6,5},{9,10},{10,9},{11,12},{12,11},... | collective-permute-start | bytes 393224 | tf_op jit(solution)/shard_map/ppermute | solution.py:310
  25.1 10.6 %collective-permute-start.7 = (f32[6,32,256]{2,1,0:T(8,128)S(1)}, f32[6,32,256]{2,1,0:T(8,128)S(1)}, u32[]{:S(2)}, u32[]{:S(2)}) collective-permute-start(f32[6,32,256]{2,1,0:T(8,128)S(1)} %get-tuple-element.64), channel_id=1, source_target_pairs={{0,8},{8,0},{16,24},{24,16},{1,9},{9,1},{17,25},{25,17},{2,10},{10... | collective-permute-start | bytes 589832 | tf_op jit(solution)/shard_map/ppermute | solution.py:309
  32.1 3.7 %collective-permute-start.6 = (f32[6,32,256]{2,1,0:T(8,128)S(1)}, f32[6,32,256]{2,1,0:T(8,128)S(1)}, u32[]{:S(2)}, u32[]{:S(2)}) collective-permute-start(f32[6,32,256]{2,1,0:T(8,128)S(1)} %get-tuple-element.65), channel_id=1, source_target_pairs={{8,16},{16,8},{9,17},{17,9},{10,18},{18,10},{11,19},{19,11},{12,20... | collective-permute-start | bytes 589832 | tf_op jit(solution)/shard_map/ppermute | solution.py:310
where the time goes:
time: 73.7 us; the launch traced here: 74 us
  blocking collectives  35 us (47%)
  Pallas kernels  19.8 us (27%)
  starting transfers between devices  14.8 us (20%)
  local copies, waits for them, and re-layouts  2.66 us (4%)
  between operations  0.86 us (1%)
    all_to_all x1, blocking collectives, per_device(): moments = lax.all_to_all(moments, ('region', 'tile'), 0, 0)  35 us
    pallas_call x8, Pallas kernels, on_device(): pl.pallas_call(kernel, out_shape=tuple(outputs), in_specs=[smem if listed...  19.8 us
    ppermute x4, starting transfers between devices, swapped(): got_up = lax.ppermute(jnp.where(even, last, first), axis, swap_up)  12.2 us
    ppermute x4, starting transfers between devices, swapped(): got_down = lax.ppermute(jnp.where(even, first, last), axis, swap_down)  2.64 us
    unnamed x5, local copies, waits for them, and re-layouts  2.59 us
  transfers between devices with their start and end apart: 8, of which 1 were waited for; matrix products, arithmetic and copies ran while one was open for 1% of the time, Pallas kernels for 20%

commit v1 on v0

--- a/solution.py
+++ b/solution.py
@@ -109,11 +109,11 @@
 
 
 def list_items(items_ref, candidates, pair_ref):
-    cols = pair_ref.shape[2]
+    cols = pair_ref.shape[1]
     count = jnp.int32(0)
     for k, own, code in candidates:
         items_ref[count + 1] = code
-        count = count + jnp.where(pair_ref[k, own // cols, own % cols] > 0, 1, 0)
+        count = count + jnp.where(pair_ref[own // cols, own % cols, k] > 0, 1, 0)
     items_ref[0] = count
     items_ref[count + 1] = NO_ITEM
 
@@ -146,30 +146,35 @@
     return found
 
 
-def pack_kernel(v_ref, c_ref, first_ref, last_ref, edge_ref, v_out_ref, c_out_ref):
-    rows, cols, rhs = v_ref.shape[:3]
+def pack_kernel(v_hbm, c_hbm, pair_hbm, first_ref, last_ref, edge_ref, v_ref, c_ref, pair_ref, sems):
+    rows, cols, rhs = v_hbm.shape[:3]
+    fetches = []
+    for row in range(rows):
+        own = pl.ds(row * cols, cols)
+        fetches.append(pltpu.make_async_copy(v_hbm.at[row], v_ref.at[own], sems.at[2 * row]))
+        fetches.append(pltpu.make_async_copy(c_hbm.at[row], c_ref.at[own], sems.at[2 * row + 1]))
+    fetches.append(pltpu.make_async_copy(pair_hbm, pair_ref, sems.at[2 * rows]))
+    for fetch in fetches:
+        fetch.start()
+    for fetch in fetches:
+        fetch.wait()
     both = slice(rhs, rhs + 2)
-    for column_ref, at in ((first_ref, 0), (last_ref, cols - 1)):
-        column_ref[:, 0:rhs] = v_ref[:, at]
-        column_ref[:, both] = c_ref[:, at]
-    for n, at in enumerate((0, rows - 1)):
-        edge_ref[n, :, 0:rhs] = v_ref[at]
-        edge_ref[n, :, both] = c_ref[at]
     for row in range(rows):
-        v_out_ref[row * cols : (row + 1) * cols] = v_ref[row]
-        c_out_ref[row * cols : (row + 1) * cols] = c_ref[row]
-
-
-def prepare_kernel(pair_ref, v_ref, c_ref, near_ref, cross_ref, parts_ref, points_ref, spread_ref):
-    rows, cols = pair_ref.shape[1:]
-    lanes = spread_ref.shape[3]
+        for column_ref, at in ((first_ref, row * cols), (last_ref, row * cols + cols - 1)):
+            column_ref[row, 0:rhs] = v_ref[at]
+            column_ref[row, both] = c_ref[at]
+    for n, row in enumerate((0, rows - 1)):
+        own = slice(row * cols, (row + 1) * cols)
+        edge_ref[n, :, 0:rhs] = v_ref[own]
+        edge_ref[n, :, both] = c_ref[own]
+
+
+def prepare_kernel(pair_ref, v_ref, c_ref, near_ref, cross_ref, parts_ref, points_ref):
+    rows, cols = pair_ref.shape[:2]
 
     def one(at, carry):
         store_parts(parts_ref, at, v_ref[at])
-        scaled = c_ref[at] * UNIT
-        points_ref[at] = scaled
-        for axis in range(2):
-            spread_ref[at, axis] = across_lanes(scaled[axis : axis + 1], lanes)
+        points_ref[at] = c_ref[at] * UNIT
         return carry
 
     lax.fori_loop(0, rows * cols, one, 0, unroll=2)
@@ -192,11 +197,13 @@
     out_ref[own] += product(dot_nt, parts_ref, other, high, low)
 
 
-def near_first_kernel(items_ref, v_ref, parts_ref, points_ref, spread_ref, out_ref, kept_ref):
+def near_first_kernel(items_ref, v_ref, parts_ref, points_ref, out_ref, kept_ref, spread_ref):
     blocks = parts_ref.shape[0]
     out_ref[...] = NUGGET * v_ref[...]
 
     def make_own(at):
+        for axis in range(2):
+            spread_ref[at, axis] = across_lanes(points_ref[at, axis : axis + 1], spread_ref.shape[3])
         make_tile(kept_ref, at, spread_ref, at, points_ref, at, 0.0, 0.0)
 
     def make_pair(n):
@@ -311,13 +318,14 @@
     return jnp.where(even, got_down, got_up), jnp.where(even, got_up, got_down)
 
 
-def on_device(kernel, outputs, inputs, scratch=(), listed=False, products=0, made=0):
+def on_device(kernel, outputs, inputs, scratch=(), listed=False, products=0, made=0, where=pltpu.VMEM):
     vmem = pl.BlockSpec(memory_space=pltpu.VMEM)
     smem = pl.BlockSpec(memory_space=pltpu.SMEM)
+    source = pl.BlockSpec(memory_space=where)
     return pl.pallas_call(
         kernel,
         out_shape=tuple(outputs),
-        in_specs=[smem if listed and n == 0 else vmem for n in range(len(inputs))],
+        in_specs=[smem if listed and n == 0 else source for n in range(len(inputs))],
         out_specs=tuple(smem if out.dtype == jnp.int32 else vmem for out in outputs),
         scratch_shapes=list(scratch),
         compiler_params=pltpu.CompilerParams(vmem_limit_bytes=VMEM_LIMIT),
@@ -333,6 +341,7 @@
 
 
 def per_device(right_side, coords, pair_list):
+    pair_list = jnp.transpose(pair_list, (1, 2, 0))
     rows, cols, rhs, points = right_side.shape
     blocks = rows * cols
     devices = lax.axis_size("region") * lax.axis_size("tile")
@@ -352,22 +361,28 @@
         bottom = jnp.concatenate([west[rows - 1 :], last, east[rows - 1 :]], axis=0)
         return swapped(top, bottom, "region")
 
-    first, last, edges, w0, stations = on_device(
-        pack_kernel, (column, column, array((2, cols, rhs + 2, points), f32), field, array((blocks, 2, points), f32)),
-        (right_side, coords),
+    fetched = (
+        column, column, array((2, cols, rhs + 2, points), f32), field, array((blocks, 2, points), f32),
+        array(pair_list.shape, i32),
+    )
+    first, last, edges, w0, stations, pairs = on_device(
+        pack_kernel, fetched,
+        tuple(pltpu.with_memory_space_constraint(x, pltpu.HBM) for x in (right_side, coords, pair_list)),
+        (pltpu.SemaphoreType.DMA((2 * rows + 1,)),), where=pltpu.HBM,
     )
     west, east = swapped(first, last, "tile")
-    near_items, cross_items, parts, own_points, spread = on_device(
+    near_items, cross_items, parts, own_points = on_device(
         prepare_kernel,
         (array((near_count + 3,), i32), array((cross_count + 3,), i32), array((blocks, 2 * rhs, points), bf16),
-         array((blocks, 2, points), f32), array((blocks, 2, points, lanes), f32)),
-        (pair_list, w0, stations), listed=True, products=blocks * each,
+         array((blocks, 2, points), f32)),
+        (pairs, w0, stations), listed=True, products=blocks * each,
     )
     west, east, parts = lax.optimization_barrier((west, east, parts))
     north, south = rows_round(edges[0], edges[1], west, east)
-    part, near_tiles = on_device(
-        near_first_kernel, (field, tiles(blocks + near_count + 2, points)),
-        (near_items, w0, parts, own_points, spread), (), True,
+    part, near_tiles, spread = on_device(
+        near_first_kernel,
+        (field, tiles(blocks + near_count + 2, points), array((blocks, 2, points, lanes), f32)),
+        (near_items, w0, parts, own_points), (), True,
         (blocks + near_count) * each, (blocks + near_count) * 2 * points * points,
     )
     w1, cross_tiles = on_device(

time: 73.7 us -> 76.9 us (1.043)
  blocking collectives: 35 us -> 38.8 us
  starting transfers between devices: 14.8 us -> 17.9 us
  local copies, waits for them, and re-layouts: 2.66 us -> 0.08 us
  Pallas kernels: 19.8 us -> 18.3 us
  waiting for transfers between devices: 0.57 us -> 1.63 us
    all_to_all x1, blocking collectives: 35 us -> 38.8 us  [per_device(): moments = lax.all_to_all(moments, ('region', 'tile'), 0, 0)]
    ppermute x4, starting transfers between devices: 12.2 us -> 15.2 us  [swapped(): got_up = lax.ppermute(jnp.where(even, last, first), axis, swap_up)]
    unnamed x5 -> x0, local copies, waits for them, and re-layouts: 2.59 us -> none
    pallas_call x8, Pallas kernels: 19.8 us -> 18.3 us  [on_device(): pl.pallas_call(kernel, out_shape=tuple(outputs), in_specs=[smem if listed...]
    ppermute x4, waiting for transfers between devices: 0.55 us -> 1.62 us  [swapped(): got_up = lax.ppermute(jnp.where(even, last, first), axis, swap_up)]
  transfers between devices with their start and end apart: 8 -> 8, of which waited for: 1 -> 1; matrix products, arithmetic and copies ran while one was open for 1% -> 0% of each run, Pallas kernels for 20% -> 14%
where the time goes in v1:
time: 76.9 us; the launch traced here: 77.8 us
  blocking collectives  38.8 us (50%)
  Pallas kernels  18.3 us (24%)
  starting transfers between devices  17.9 us (23%)
  waiting for transfers between devices  1.63 us (2%)
  between operations  0.86 us (1%)
    all_to_all x1, blocking collectives, per_device(): moments = lax.all_to_all(moments, ('region', 'tile'), 0, 0)  38.8 us
    pallas_call x8, Pallas kernels, on_device(): pl.pallas_call(kernel, out_shape=tuple(outputs), in_specs=[smem if listed...  18.3 us
    ppermute x4, starting transfers between devices, swapped(): got_up = lax.ppermute(jnp.where(even, last, first), axis, swap_up)  15.2 us
    ppermute x4, starting transfers between devices, swapped(): got_down = lax.ppermute(jnp.where(even, first, last), axis, swap_down)  2.64 us
    ppermute x4, waiting for transfers between devices, swapped(): got_up = lax.ppermute(jnp.where(even, last, first), axis, swap_up)  1.62 us
  transfers between devices with their start and end apart: 8, of which 1 were waited for; matrix products, arithmetic and copies ran while one was open for 0% of the time, Pallas kernels for 14%

profile of v1, /device:TPU:0, one launch (start us, length us, event | category | flops | bytes accessed | tf_op | source)
XLA Modules:
  0.0 77.8 jit_solution(17305084205254888419)
XLA Ops:
  0.6 2.0 %pack_kernel.1 = (f32[4,34,256]{2,1,0:T(8,128)S(1)}, f32[4,34,256]{2,1,0:T(8,128)S(1)}, f32[2,4,34,256]{3,2,1,0:T(8,128)S(1)}, f32[16,32,256]{2,1,0:T(8,128)S(1)...) custom-call(f32[4,4,32,256]{3,2,1,0:T(8,128)} %v_hbm.1, f32[4,4,2,256]{3,2,1,0:T(2,128)} %c_hbm.1, s32[4,4,8]{2,1,0:T(4,128)} %bitcast.25), custom_call_target="tpu_custom_call" | custom-call | bytes 557568 | tf_op jit(solution)/shard_map/pack_kernel/pallas_call | solution.py:325
  2.7 0.6 collective-permute-start.1
  3.2 0.7 collective-permute-start
  3.9 1.6 %prepare_kernel.1 = (s32[45]{0:T(128)S(1)}, s32[47]{0:T(128)S(1)}, bf16[16,64,256]{2,1,0:T(8,128)(2,1)S(1)}, f32[16,2,256]{2,1,0:T(2,128)S(1)}) custom-call(s32[4,4,8]{2,1,0:T(4,128)S(1)} %get-tuple-element.29.pair_ref, f32[16,32,256]{2,1,0:T(8,128)S(1)} %get-tuple-element.30.v_ref.v0_ref, f32[16,2,256]{2,1,0:T(2,128)S(1)} %get-tuple-element.31.c_ref), custom_call_target="tpu_custom_call" | custom-call | flops 201326592 | bytes 557568 | tf_op jit(solution)/shard_map/prepare_kernel/pallas_call | solution.py:325
  5.5 0.0 collective-permute-done.1
  5.5 0.0 collective-permute-done
  5.7 2.6 %collective-permute-start.3 = (f32[6,34,256]{2,1,0:T(8,128)S(1)}, f32[6,34,256]{2,1,0:T(8,128)S(1)}, u32[]{:S(2)}, u32[]{:S(2)}) collective-permute-start(f32[6,34,256]{2,1,0:T(8,128)S(1)} %get-tuple-element.62), channel_id=1, source_target_pairs={{0,8},{8,0},{16,24},{24,16},{1,9},{9,1},{17,25},{25,17},{2,10},{10... | collective-permute-start | bytes 626696 | tf_op jit(solution)/shard_map/ppermute | solution.py:316
  8.2 0.7 collective-permute-start.2
  8.9 6.6 %near_first_kernel.1 = (f32[16,32,256]{2,1,0:T(8,128)S(1)}, bf16[60,2,256,256]{3,2,1,0:T(8,128)(2,1)S(1)}, f32[16,2,256,128]{3,2,1,0:T(8,128)S(1)}) custom-call(s32[45]{0:T(128)S(1)} %get-tuple-element.33.items_ref, f32[16,32,256]{2,1,0:T(8,128)S(1)} %get-tuple-element.30.v_ref.v0_ref, bf16[16,64,256]{2,1,0:T(8,128)(2,1)S(1)} %get-tuple-element.37.parts_ref, ...), custom_call_target="tpu_custom_call" | custom-call | flops 729808896 | bytes 1605812 | tf_op jit(solution)/shard_map/near_first_kernel/pallas_call | solution.py:325
  15.5 0.0 collective-permute-done.3
  15.5 0.0 collective-permute-done.2
  15.6 2.3 %cross_first_kernel.1 = (f32[16,32,256]{2,1,0:T(8,128)S(1)}, bf16[46,2,256,256]{3,2,1,0:T(8,128)(2,1)S(1)}) custom-call(s32[47]{0:T(128)S(1)} %get-tuple-element.32.items_ref, f32[16,32,256]{2,1,0:T(8,128)S(1)} %get-tuple-element.39.sum_ref, f32[4,34,256]{2,1,0:T(8,128)S(1)} %get-tuple-element.40.west_ref, f32[4,34,256]{2,1,0:T(8,128)S(1)} %get-tuple-element.41.east_ref, ...), custom_call_target="tpu_custom_call" | custom-call | flops 553648128 | bytes 5415100 | tf_op jit(solution)/shard_map/cross_first_kernel/pallas_call | solution.py:325
  17.9 7.2 %collective-permute-start.5 = (f32[4,32,256]{2,1,0:T(8,128)S(1)}, f32[4,32,256]{2,1,0:T(8,128)S(1)}, u32[]{:S(2)}, u32[]{:S(2)}) collective-permute-start(f32[4,32,256]{2,1,0:T(8,128)S(1)} %get-tuple-element.58), channel_id=1, source_target_pairs={{0,1},{1,0},{2,3},{3,2},{4,5},{5,4},{6,7},{7,6},{8,9},{9,8},{10,11... | collective-permute-start | bytes 393224 | tf_op jit(solution)/shard_map/ppermute | solution.py:316
  25.2 0.7 collective-permute-start.4
  25.8 1.0 %own_again_kernel.1 = (f32[16,32,256]{2,1,0:T(8,128)S(1)}, bf16[16,64,256]{2,1,0:T(8,128)(2,1)S(1)}) custom-call(f32[16,32,256]{2,1,0:T(8,128)S(1)} %get-tuple-element.44.v_ref.v1_ref, bf16[60,2,256,256]{3,2,1,0:T(8,128)(2,1)S(1)} %get-tuple-element.45.kept_ref), custom_call_target="tpu_custom_call" | custom-call | flops 201326592 | bytes 31981568 | tf_op jit(solution)/shard_map/own_again_kernel/pallas_call | solution.py:325
  26.9 0.0 collective-permute-done.5
  26.9 0.0 collective-permute-done.4
  27.0 4.9 %collective-permute-start.7 = (f32[6,32,256]{2,1,0:T(8,128)S(1)}, f32[6,32,256]{2,1,0:T(8,128)S(1)}, u32[]{:S(2)}, u32[]{:S(2)}) collective-permute-start(f32[6,32,256]{2,1,0:T(8,128)S(1)} %get-tuple-element.66), channel_id=1, source_target_pairs={{0,8},{8,0},{16,24},{24,16},{1,9},{9,1},{17,25},{25,17},{2,10},{10... | collective-permute-start | bytes 589832 | tf_op jit(solution)/shard_map/ppermute | solution.py:316
  31.9 0.7 collective-permute-start.6
  32.6 1.4 %inner_again_kernel.1.sum_ref = f32[16,32,256]{2,1,0:T(8,128)S(1)} custom-call(s32[45]{0:T(128)S(1)} %get-tuple-element.33.items_ref, f32[16,32,256]{2,1,0:T(8,128)S(1)} %get-tuple-element.47.sum_ref, bf16[16,64,256]{2,1,0:T(8,128)(2,1)S(1)} %get-tuple-element.48.parts_ref, bf16[60,2,256,256]{3,2,1,0:T(8,128)(2,1)S(1)} %get-tuple-element.45.kept_ref), custom_call_target="tpu_custom_call" | custom-call | flops 528482304 | bytes 33030324 | tf_op jit(solution)/shard_map/inner_again_kernel/pallas_call | solution.py:325
  34.0 1.6 %collective-permute-done.7 = f32[6,32,256]{2,1,0:T(8,128)S(1)} collective-permute-done((f32[6,32,256]{2,1,0:T(8,128)S(1)}, f32[6,32,256]{2,1,0:T(8,128)S(1)}, u32[]{:S(2)}, u32[]{:S(2)}) %collective-permute-start.7) | collective-permute-done | bytes 196640 | tf_op jit(solution)/shard_map/ppermute | solution.py:316
  35.6 0.0 collective-permute-done.6
  35.6 2.1 %cross_again_kernel.1 = (f32[16,32,256]{2,1,0:T(8,128)S(1)}, f32[32,1,128]{2,1,0:T(1,128)S(1)}) custom-call(s32[47]{0:T(128)S(1)} %get-tuple-element.32.items_ref, f32[16,32,256]{2,1,0:T(8,128)S(1)} %inner_again_kernel.1.sum_ref, f32[4,32,256]{2,1,0:T(8,128)S(1)} %get-tuple-element.49.west_ref, f32[4,32,256]{2,1,0:T(8,128)S(1)} %get-tuple-element.50.east_ref, ...), custom_call_target="tpu_custom_call" | custom-call | flops 553648128 | bytes 26345660 | tf_op jit(solution)/shard_map/cross_again_kernel/pallas_call | solution.py:325
  37.7 38.8 %all_to_all.5.moments_ref = f32[32,1,128]{2,1,0:T(1,128)S(1)} all-to-all(f32[32,1,128]{2,1,0:T(1,128)S(1)} %get-tuple-element.52), channel_id=1, replica_groups=mesh['region'=4,'tile'=8] {'region','tile'}, dimensions={0} | all-to-all | bytes 32768 | tf_op jit(solution)/shard_map/all_to_all | solution.py:408
  76.5 1.3 %final_kernel.1 = (f32[16,32,256]{2,1,0:T(8,128)}, f32[16,32,256]{2,1,0:T(8,128)}) custom-call(f32[32,1,128]{2,1,0:T(1,128)S(1)} %all_to_all.5.moments_ref, f32[16,32,256]{2,1,0:T(8,128)S(1)} %get-tuple-element.30.v_ref.v0_ref, f32[16,32,256]{2,1,0:T(8,128)S(1)} %get-tuple-element.44.v_ref.v1_ref, f32[16,32,256]{2,1,0:T(8,128)S(1)} %get-tuple-element.53.v2_ref), custom_call_target="tpu_custom_call" | custom-call | bytes 1589248 | tf_op jit(solution)/shard_map/final_kernel/pallas_call | solution.py:325
  (13 shorter events, 0.3 us)
Async XLA Ops:
  2.7 2.9 %collective-permute-start.1 = (f32[4,34,256]{2,1,0:T(8,128)S(1)}, f32[4,34,256]{2,1,0:T(8,128)S(1)}, u32[]{:S(2)}, u32[]{:S(2)}) collective-permute-start(f32[4,34,256]{2,1,0:T(8,128)S(1)} %get-tuple-element.72), channel_id=1, source_target_pairs={{0,1},{1,0},{2,3},{3,2},{4,5},{5,4},{6,7},{7,6},{8,9},{9,8},{10,11... | collective-permute-start | bytes 417800 | tf_op jit(solution)/shard_map/ppermute | solution.py:316
  3.2 2.3 %collective-permute-start = (f32[4,34,256]{2,1,0:T(8,128)S(1)}, f32[4,34,256]{2,1,0:T(8,128)S(1)}, u32[]{:S(2)}, u32[]{:S(2)}) collective-permute-start(f32[4,34,256]{2,1,0:T(8,128)S(1)} %get-tuple-element.73), channel_id=1, source_target_pairs={{1,2},{2,1},{3,4},{4,3},{5,6},{6,5},{9,10},{10,9},{11,12},{12,11},... | collective-permute-start | bytes 417800 | tf_op jit(solution)/shard_map/ppermute | solution.py:317
  5.7 9.9 %collective-permute-start.3 = (f32[6,34,256]{2,1,0:T(8,128)S(1)}, f32[6,34,256]{2,1,0:T(8,128)S(1)}, u32[]{:S(2)}, u32[]{:S(2)}) collective-permute-start(f32[6,34,256]{2,1,0:T(8,128)S(1)} %get-tuple-element.62), channel_id=1, source_target_pairs={{0,8},{8,0},{16,24},{24,16},{1,9},{9,1},{17,25},{25,17},{2,10},{10... | collective-permute-start | bytes 626696 | tf_op jit(solution)/shard_map/ppermute | solution.py:316
  8.2 7.3 %collective-permute-start.2 = (f32[6,34,256]{2,1,0:T(8,128)S(1)}, f32[6,34,256]{2,1,0:T(8,128)S(1)}, u32[]{:S(2)}, u32[]{:S(2)}) collective-permute-start(f32[6,34,256]{2,1,0:T(8,128)S(1)} %get-tuple-element.63), channel_id=1, source_target_pairs={{8,16},{16,8},{9,17},{17,9},{10,18},{18,10},{11,19},{19,11},{12,20... | collective-permute-start | bytes 626696 | tf_op jit(solution)/shard_map/ppermute | solution.py:317
  17.9 9.0 %collective-permute-start.5 = (f32[4,32,256]{2,1,0:T(8,128)S(1)}, f32[4,32,256]{2,1,0:T(8,128)S(1)}, u32[]{:S(2)}, u32[]{:S(2)}) collective-permute-start(f32[4,32,256]{2,1,0:T(8,128)S(1)} %get-tuple-element.58), channel_id=1, source_target_pairs={{0,1},{1,0},{2,3},{3,2},{4,5},{5,4},{6,7},{7,6},{8,9},{9,8},{10,11... | collective-permute-start | bytes 393224 | tf_op jit(solution)/shard_map/ppermute | solution.py:316
  25.2 1.7 %collective-permute-start.4 = (f32[4,32,256]{2,1,0:T(8,128)S(1)}, f32[4,32,256]{2,1,0:T(8,128)S(1)}, u32[]{:S(2)}, u32[]{:S(2)}) collective-permute-start(f32[4,32,256]{2,1,0:T(8,128)S(1)} %get-tuple-element.59), channel_id=1, source_target_pairs={{1,2},{2,1},{3,4},{4,3},{5,6},{6,5},{9,10},{10,9},{11,12},{12,11},... | collective-permute-start | bytes 393224 | tf_op jit(solution)/shard_map/ppermute | solution.py:317
  27.0 8.5 %collective-permute-start.7 = (f32[6,32,256]{2,1,0:T(8,128)S(1)}, f32[6,32,256]{2,1,0:T(8,128)S(1)}, u32[]{:S(2)}, u32[]{:S(2)}) collective-permute-start(f32[6,32,256]{2,1,0:T(8,128)S(1)} %get-tuple-element.66), channel_id=1, source_target_pairs={{0,8},{8,0},{16,24},{24,16},{1,9},{9,1},{17,25},{25,17},{2,10},{10... | collective-permute-start | bytes 589832 | tf_op jit(solution)/shard_map/ppermute | solution.py:316
  31.9 3.7 %collective-permute-start.6 = (f32[6,32,256]{2,1,0:T(8,128)S(1)}, f32[6,32,256]{2,1,0:T(8,128)S(1)}, u32[]{:S(2)}, u32[]{:S(2)}) collective-permute-start(f32[6,32,256]{2,1,0:T(8,128)S(1)} %get-tuple-element.67), channel_id=1, source_target_pairs={{8,16},{16,8},{9,17},{17,9},{10,18},{18,10},{11,19},{19,11},{12,20... | collective-permute-start | bytes 589832 | tf_op jit(solution)/shard_map/ppermute | solution.py:317
